TPU v7x, 128 devices: a whole 4x4x4 slice. The times are simulated.
128 devices in a mesh: corpus: 16 (over z, y), fsdp: 2 (over core), tensor: 4 (over x).
Axes of the slice: x: 4, y: 4, z: 4, core: 2. Of those that a mesh axis runs over, the one named last changes fastest.
Arguments:
- queries_in: bfloat16 [4096, 4096], P(('corpus', 'fsdp')), may hold values from -6 to 6
- head_weight: bfloat16 [4096, 4096], P('fsdp', 'tensor'), may hold values from -0.09375 to 0.09375
- passages: bfloat16 [16384, 4096], P('corpus', 'tensor'), may hold values from -0.15625 to 0.15625
- teacher: float32 [4096, 4, 32], P(('corpus', 'fsdp')), may hold values from -250 to 400
- cand_block: int32 [4096, 4], P(('corpus', 'fsdp')), may hold values from 0 to 127, all different within a row; in each aligned block of 128 rows (0 to 127, 128 to 255, ...) at most 6 rows name the same one
- cand_offset: int32 [4096, 4, 32], P(('corpus', 'fsdp')), may hold values from 0 to 127, as said below
- block_slot: int32 [128], replicated, may hold values from 0 to 127, each once
Outputs:
- kl_loss: float32 [4096], P(('corpus', 'fsdp'))
- head_grad: float32 [4096, 4096], P('fsdp', 'tensor')
Inputs may be any that keep to these rules, and one draw needn't show every extreme that they name: `cand_block`: in the rows of one device no block id appears more than 6 times, and some block id appears exactly 6 times there; the 4 ids of one query differ. `cand_offset`: the 32 offsets of one query in one block differ. `block_slot`: each storage position is taken by exactly one block.
All inputs are finite; a program needn't handle non-finite values.
Results may differ from a plain program's by a relative error of at most 0.012.
The roundings to bfloat16 on the way count: a program that leaves them out, or rounds other values in their place, can miss the bound.
Values may be sent and summed in bfloat16 or wider, within the bound.
A program may use at most 128 MiB of HBM per device.

v0:
```python
import jax
import jax.numpy as jnp
from jax import lax
from jax.sharding import PartitionSpec as P

ROWS = 128
MOSTB = 6
SWAP = [(0, 1), (1, 0)]


def on_device(queries_in, head_weight, passages, teacher, cand_block, cand_offset, block_slot):
    query_rows, width = queries_in.shape
    half = width // 2
    cols = head_weight.shape[1]
    per_query = cand_block.shape[1]
    offset_count = cand_offset.shape[2]
    total_blocks = block_slot.shape[0]
    n_corpus = lax.axis_size("corpus")
    blocks_here = passages.shape[0] // ROWS
    slot_total = total_blocks * MOSTB
    slots_each = blocks_here * MOSTB
    picks = query_rows * per_query
    first = lax.axis_index("fsdp") == 0
    low, high = (queries_in[:, :half], queries_in[:, half:])
    mine = jnp.where(first, low, high)
    other = jnp.where(first, high, low)
    theirs = lax.ppermute(other, "fsdp", SWAP)
    part_theirs = jnp.dot(theirs, head_weight, preferred_element_type=jnp.float32)
    back = lax.ppermute(part_theirs, "fsdp", SWAP)
    part_mine = jnp.dot(mine, head_weight, preferred_element_type=jnp.float32)
    query = (part_mine + back).astype(jnp.bfloat16)
    all_mine = lax.all_gather(mine, "corpus", axis=0, tiled=True)
    all_theirs = lax.all_gather(theirs, "corpus", axis=0, tiled=True)
    block_ids = lax.broadcasted_iota(jnp.int32, (1, total_blocks), 1)
    named = (cand_block.reshape(-1, 1) == block_ids).astype(jnp.int32)
    slot_of = jnp.sum(named * block_slot.reshape(1, -1), axis=1)
    hits = slot_of[:, None] == block_ids
    before = (
        lax.broadcasted_iota(jnp.int32, (picks, picks), 1)
        < lax.broadcasted_iota(jnp.int32, (picks, picks), 0)
    ).astype(jnp.bfloat16)
    earlier = jnp.dot(before, hits.astype(jnp.bfloat16), preferred_element_type=jnp.float32)
    slot_rank = jnp.sum(jnp.where(hits, earlier, 0.0), axis=1).astype(jnp.int32)
    position = slot_of * MOSTB + slot_rank
    slot_ids = lax.broadcasted_iota(jnp.int32, (slot_total, 1), 0)
    place = (slot_ids == position.reshape(1, -1)).astype(jnp.bfloat16)
    by_query = position.reshape(query_rows, per_query)
    owner = slot_ids == by_query[:, 0].reshape(1, -1)
    for g in range(1, per_query):
        owner = owner | (slot_ids == by_query[:, g].reshape(1, -1))
    owner = owner.astype(jnp.bfloat16)
    slot_block = slot_ids % slots_each // MOSTB
    send_queries = jnp.dot(owner, query, preferred_element_type=jnp.float32).astype(jnp.bfloat16)
    got_queries = lax.all_to_all(
        send_queries.reshape(n_corpus, slots_each, cols), "corpus", 0, 0, tiled=True
    ).reshape(slot_total, cols)
    wide = lax.dot_general(
        got_queries, passages, (((1,), (1,)), ((), ())), preferred_element_type=jnp.float32
    )
    scores = wide[:, :ROWS]
    for j in range(1, blocks_here):
        scores = jnp.where(slot_block == j, wide[:, j * ROWS : (j + 1) * ROWS], scores)
    returned = lax.all_to_all(
        scores.reshape(n_corpus, slots_each, ROWS), "corpus", 0, 0, tiled=True
    ).reshape(slot_total, ROWS)
    picked = returned[position]
    offsets = cand_offset.reshape(picks, offset_count)
    row_ids = lax.broadcasted_iota(jnp.int32, (1, 1, ROWS), 2)
    chosen = offsets[:, :, None] == row_ids
    partial = jnp.sum(jnp.where(chosen, picked[:, None, :], 0.0), axis=2)
    total = partial.reshape(query_rows, per_query * offset_count)
    total = total + lax.ppermute(total, "tensor", [(0, 1), (1, 0), (2, 3), (3, 2)])
    total = total + lax.ppermute(total, "tensor", [(0, 2), (2, 0), (1, 3), (3, 1)])
    student = 50.0 * total
    cached = teacher.reshape(query_rows, per_query * offset_count)
    log_student = student - jax.nn.logsumexp(student, axis=1, keepdims=True)
    log_teacher = cached - jax.nn.logsumexp(cached, axis=1, keepdims=True)
    prob_teacher = jnp.exp(log_teacher)
    kl_loss = jnp.sum(prob_teacher * (log_teacher - log_student), axis=1)
    dscore = (50.0 * (jnp.exp(log_student) - prob_teacher)).astype(jnp.bfloat16)
    spread = jnp.sum(
        jnp.where(chosen, dscore.reshape(picks, offset_count, 1).astype(jnp.float32), 0.0), axis=1
    ).astype(jnp.bfloat16)
    dense = jnp.dot(place, spread, preferred_element_type=jnp.float32).astype(jnp.bfloat16)
    got_dense = lax.all_to_all(
        dense.reshape(n_corpus, slots_each, ROWS), "corpus", 0, 0, tiled=True
    ).reshape(slot_total, ROWS)
    expanded = jnp.concatenate(
        [jnp.where(slot_block == j, got_dense, jnp.bfloat16(0)) for j in range(blocks_here)], axis=1
    )
    block_part = jnp.dot(expanded, passages, preferred_element_type=jnp.float32).astype(
        jnp.bfloat16
    )
    arrived = lax.all_to_all(
        block_part.reshape(n_corpus, slots_each, cols), "corpus", 0, 0, tiled=True
    ).reshape(slot_total, cols)
    query_grad = lax.dot_general(
        owner, arrived, (((0,), (0,)), ((), ())), preferred_element_type=jnp.float32
    ).astype(jnp.bfloat16)
    grad_mine = lax.all_gather(query_grad, "corpus", axis=0, tiled=True)
    grad_theirs = lax.ppermute(grad_mine, "fsdp", SWAP)
    across = (((0,), (0,)), ((), ()))
    head_grad = lax.dot_general(
        all_mine, grad_mine, across, preferred_element_type=jnp.float32
    ) + lax.dot_general(all_theirs, grad_theirs, across, preferred_element_type=jnp.float32)
    return (kl_loss, head_grad)


def solution(mesh):
    placed = (
        P(("corpus", "fsdp"), None),
        P("fsdp", "tensor"),
        P("corpus", "tensor"),
        P(("corpus", "fsdp"), None, None),
        P(("corpus", "fsdp"), None),
        P(("corpus", "fsdp"), None, None),
        P(),
    )
    return jax.shard_map(
        on_device,
        mesh=mesh,
        in_specs=placed,
        out_specs=(P(("corpus", "fsdp")), P("fsdp", "tensor")),
        check_vma=False,
    )
```

profile of v0, /device:TPU:1, one launch (start us, length us, event | category | flops | bytes accessed | tf_op | source)
XLA Modules:
  0.0 353.7 jit_solution(15698942265412292982)
XLA Ops:
  7.2 0.0 copy-start
  7.2 2.2 broadcast_select_fusion
  9.4 1.4 collective-permute-start
  10.8 0.0 copy-done.6
  10.8 0.1 copy.18
  10.9 0.1 eq.213
  11.0 1.5 collective-permute-done
  12.5 3.9 %fusion.26 = f32[128,1024]{1,0:T(8,128)} fusion(bf16[128,2048]{1,0:T(8,128)(2,1)S(1)} %collective-permute-done, bf16[2048,1024]{1,0:T(8,128)(2,1)} %param.8), kind=kOutput, calls=%fused_computation.91 | convolution fusion | flops 536870912 | bytes 5242880 | tf_op jit(solution)/shard_map/dot_general | solution.py:28
  16.5 0.0 copy-done.3
  16.5 0.4 collective-permute-start.1
  16.8 0.2 select_reduce_fusion.2
  17.1 0.3 fusion.2
  17.4 0.1 add.152
  17.5 0.2 slice_reduce_fusion.3
  17.8 1.0 collective-permute-done.1
  18.7 4.6 %convolution_convert_fusion = bf16[768,1024]{1,0:T(8,128)(2,1)} fusion(f32[128,1024]{1,0:T(8,128)} %collective-permute-done.1, s32[128]{0:T(128)S(1)} %get-tuple-element.3, s32[128]{0:T(128)S(1)} %get-tuple-element.4, s32[128]{0:T(128)S(1)} %get-tuple-element.5, s32[128]{0:T(128)S(1)} %get-tuple-element.2, bf16[128,2048]{1,0:T(8,128)(2,1)S(1)} %get-tuple-element.9, ...), kind=kOutput, calls=%fused_computation.5 | convolution fusion | flops 739934208 | bytes 6817792 | tf_op jit(solution)/shard_map/dot_general | solution.py:53
  23.3 7.9 %all-to-all-start = ((bf16[16,48,1024]{2,1,0:T(8,128)(2,1)}), bf16[16,48,1024]{2,1,0:T(8,128)(2,1)}, u32[]{:S(2)}, u32[]{:S(2)}) async-start(bf16[16,48,1024]{2,1,0:T(8,128)(2,1)} %bitcast.46), calls=%async_computation | async-start | bytes 3145728 | tf_op jit(solution)/shard_map/all_to_all | solution.py:54
  31.4 23.9 %all-to-all-done = bf16[16,48,1024]{2,1,0:T(8,128)(2,1)} async-done(((bf16[16,48,1024]{2,1,0:T(8,128)(2,1)}), bf16[16,48,1024]{2,1,0:T(8,128)(2,1)}, u32[]{:S(2)}, u32[]{:S(2)}) %all-to-all-start) | async-done | bytes 1572896 | tf_op jit(solution)/shard_map/all_to_all | solution.py:54
  55.3 3.2 fusion.27
  58.5 0.0 copy-start.5
  58.6 0.0 copy-start.4
  58.6 2.1 fusion.9
  60.7 4.1 %all-to-all-start.1 = ((f32[16,48,128]{2,1,0:T(8,128)}), f32[16,48,128]{2,1,0:T(8,128)S(1)}, u32[]{:S(2)}, u32[]{:S(2)}) async-start(f32[16,48,128]{2,1,0:T(8,128)} %bitcast.4), calls=%async_computation.1 | async-start | bytes 786432 | tf_op jit(solution)/shard_map/all_to_all | solution.py:63
  64.8 0.1 copy.17
  65.0 8.7 %all-to-all-done.1 = f32[16,48,128]{2,1,0:T(8,128)S(1)} async-done(((f32[16,48,128]{2,1,0:T(8,128)}), f32[16,48,128]{2,1,0:T(8,128)S(1)}, u32[]{:S(2)}, u32[]{:S(2)}) %all-to-all-start.1) | async-done | bytes 393248 | tf_op jit(solution)/shard_map/all_to_all | solution.py:63
  73.8 1.0 gather_fusion
  74.8 5.1 %select_reduce_fusion.1 = f32[512,32]{1,0:T(8,128)S(1)} fusion(f32[512,128]{1,0:T(8,128)S(1)} %gather_fusion, s32[512,32]{1,0:T(8,128)S(1)} %bitcast.47), kind=kLoop, calls=%fused_computation.2 | loop fusion | flops 6275072 | bytes 393216 | tf_op jit(solution)/shard_map/reduce_sum | solution.py:70
  79.9 0.1 reshape.196
  80.0 0.1 copy.20
  80.1 1.3 collective-permute-start.2
  81.5 1.9 collective-permute-done.2
  83.3 2.8 collective-permute-start.3
  86.2 2.6 collective-permute-done.3
  88.8 0.6 fusion.18
  89.4 0.1 copy.21
  89.5 0.1 reshape.201
  89.6 5.6 %select_reduce_fusion = bf16[512,128]{1,0:T(8,128)(2,1)S(1)} fusion(f32[512,32]{1,0:T(8,128)S(1)} %reshape.201, s32[512,32]{1,0:T(8,128)S(1)} %bitcast.48), kind=kLoop, calls=%fused_computation.1 | loop fusion | flops 6225920 | bytes 262144 | tf_op jit(solution)/shard_map/reduce_sum | solution.py:81
  95.2 1.1 fusion.1
  96.3 3.5 all-to-all-start.2
  99.8 0.0 all-gather.6.cloned.1.call-start
  99.9 7.1 %all-to-all-done.2 = bf16[16,48,128]{2,1,0:T(8,128)(2,1)S(1)} async-done(((bf16[16,48,128]{2,1,0:T(8,128)(2,1)}), bf16[16,48,128]{2,1,0:T(8,128)(2,1)S(1)}, u32[]{:S(2)}, u32[]{:S(2)}) %all-to-all-start.2) | async-done | bytes 196640 | tf_op jit(solution)/shard_map/all_to_all | solution.py:85
  107.0 1.2 bitcast_select_fusion
  108.2 0.1 constant_dynamic-update-slice_fusion.6
  108.3 0.1 constant_dynamic-update-slice_fusion.5
  108.4 0.1 constant_dynamic-update-slice_fusion.4
  108.4 0.1 constant_dynamic-update-slice_fusion.3
  108.5 0.1 constant_dynamic-update-slice_fusion.2
  108.6 0.1 constant_dynamic-update-slice_fusion.1
  108.6 0.1 constant_dynamic-update-slice_fusion
  108.7 1.8 convolution_convert_fusion.1
  110.5 21.1 %all_to_all.20 = bf16[16,48,1024]{2,1,0:T(8,128)(2,1)S(1)} all-to-all(bf16[16,48,1024]{2,1,0:T(8,128)(2,1)S(1)} %bitcast.50), channel_id=1, replica_groups=mesh['corpus'=16,'fsdp'=2,'tensor'=4] {'corpus'}, dimensions={0} | all-to-all | bytes 3145728 | tf_op jit(solution)/shard_map/all_to_all | solution.py:94
  131.6 1.2 convolution_convert_fusion.2
  132.8 0.0 all-gather.6.cloned.1.call-update
  132.8 0.0 all-gather.4.cloned.1.call-start
  132.9 0.7 all-gather.4.cloned.1.call-update
  133.6 0.0 all-gather.8.cloned.1.call-start
  133.6 0.7 all-gather.8.cloned.1.call-update
  134.3 51.5 %all-gather.6.cloned.1.call-done = bf16[2048,1024]{1,0:T(8,128)(2,1)} async-done(((bf16[128,1024]{1,0:T(8,128)(2,1)}), bf16[2048,1024]{1,0:T(8,128)(2,1)}) %all-gather.6.cloned.1.call-update) | async-done | bytes 4194320 | tf_op jit(solution)/shard_map/all_gather | solution.py:100
  185.8 0.8 collective-permute-start.4
  186.6 71.8 %all-gather.4.cloned.1.call-done = bf16[2048,2048]{1,0:T(8,128)(2,1)} async-done(((bf16[128,2048]{1,0:T(8,128)(2,1)}), bf16[2048,2048]{1,0:T(8,128)(2,1)}) %all-gather.4.cloned.1.call-update) | async-done | bytes 8388624 | tf_op jit(solution)/shard_map/all_gather | solution.py:32
  258.5 14.6 %fusion.28 = f32[2048,1024]{1,0:T(8,128)} fusion(bf16[2048,2048]{1,0:T(8,128)(2,1)} %all-gather.4.cloned.1.call-done, bf16[2048,1024]{1,0:T(8,128)(2,1)} %all-gather.6.cloned.1.call-done), kind=kOutput, calls=%fused_computation.93 | convolution fusion | flops 8589934592 | bytes 20971520 | tf_op jit(solution)/shard_map/dot_general | solution.py:103
  273.1 58.1 %all-gather.8.cloned.1.call-done = bf16[2048,2048]{1,0:T(8,128)(2,1)} async-done(((bf16[128,2048]{1,0:T(8,128)(2,1)}), bf16[2048,2048]{1,0:T(8,128)(2,1)}) %all-gather.8.cloned.1.call-update) | async-done | bytes 8388624 | tf_op jit(solution)/shard_map/all_gather | solution.py:33
  331.2 0.0 collective-permute-done.4
  331.2 16.0 %convolution_add_fusion = f32[2048,1024]{1,0:T(8,128)} fusion(f32[2048,1024]{1,0:T(8,128)} %fusion.28, bf16[2048,2048]{1,0:T(8,128)(2,1)} %all-gather.8.cloned.1.call-done, bf16[2048,1024]{1,0:T(8,128)(2,1)} %collective-permute-done.4), kind=kOutput, calls=%fused_computation.4 | convolution fusion | flops 8592031744 | bytes 29360128 | tf_op jit(solution)/shard_map/dot_general | solution.py:105
  (29 shorter events, 0.4 us)
Async XLA Ops:
  7.2 48.1 %copy-start = (bf16[1024,1024]{1,0:T(8,128)(2,1)S(1)}, bf16[1024,1024]{1,0:T(8,128)(2,1)}, u32[]{:S(2)}) copy-start(bf16[1024,1024]{1,0:T(8,128)(2,1)} %param.9) | copy-start | bytes 6291460
  7.2 3.6 %copy-start.6 = (s32[128,4]{0,1:T(4,128)S(1)}, s32[128,4]{0,1:T(4,128)}, u32[]{:S(2)}) copy-start(s32[128,4]{0,1:T(4,128)} %param.11) | copy-start | bytes 6148
  9.4 9.3 %copy-start.2 = (bf16[128,2048]{1,0:T(8,128)(2,1)}, bf16[128,2048]{1,0:T(8,128)(2,1)S(1)}, u32[]{:S(2)}) copy-start(bf16[128,2048]{1,0:T(8,128)(2,1)S(1)} %get-tuple-element.9) | copy-start | bytes 1572868
  9.4 3.1 collective-permute-start
  12.5 3.9 %copy-start.3 = (bf16[128,2048]{1,0:T(8,128)(2,1)}, bf16[128,2048]{1,0:T(8,128)(2,1)S(1)}, u32[]{:S(2)}) copy-start(bf16[128,2048]{1,0:T(8,128)(2,1)S(1)} %collective-permute-done) | copy-start | bytes 1572868
  12.5 4.3 %copy-start.7 = (s32[128]{0:T(128)S(1)}, s32[128]{0:T(128)}, u32[]{:S(2)}) copy-start(s32[128]{0:T(128)} %param.13) | copy-start | bytes 1540
  16.5 2.3 collective-permute-start.1
  23.3 32.0 %all-to-all-start = ((bf16[16,48,1024]{2,1,0:T(8,128)(2,1)}), bf16[16,48,1024]{2,1,0:T(8,128)(2,1)}, u32[]{:S(2)}, u32[]{:S(2)}) async-start(bf16[16,48,1024]{2,1,0:T(8,128)(2,1)} %bitcast.46), calls=%async_computation | async-start | bytes 3145728 | tf_op jit(solution)/shard_map/all_to_all | solution.py:54
  58.5 6.2 %copy-start.5 = (s32[128,4,32]{0,2,1:T(8,128)S(1)}, s32[128,4,32]{0,2,1:T(8,128)}, u32[]{:S(2)}) copy-start(s32[128,4,32]{0,2,1:T(8,128)} %param.12) | copy-start | bytes 196612
  58.6 6.4 %copy-start.4 = (f32[128,4,32]{0,2,1:T(8,128)S(1)}, f32[128,4,32]{0,2,1:T(8,128)}, u32[]{:S(2)}) copy-start(f32[128,4,32]{0,2,1:T(8,128)} %param.10) | copy-start | bytes 196612
  60.7 13.1 %all-to-all-start.1 = ((f32[16,48,128]{2,1,0:T(8,128)}), f32[16,48,128]{2,1,0:T(8,128)S(1)}, u32[]{:S(2)}, u32[]{:S(2)}) async-start(f32[16,48,128]{2,1,0:T(8,128)} %bitcast.4), calls=%async_computation.1 | async-start | bytes 786432 | tf_op jit(solution)/shard_map/all_to_all | solution.py:63
  80.1 3.2 collective-permute-start.2
  83.3 5.4 %collective-permute-start.3 = (f32[128,128]{0,1:T(8,128)S(1)}, f32[128,128]{0,1:T(8,128)S(1)}, u32[]{:S(2)}, u32[]{:S(2)}) collective-permute-start(f32[128,128]{0,1:T(8,128)S(1)} %add.157), channel_id=1, source_target_pairs={{0,2},{2,0},{1,3},{3,1},{4,6},{6,4},{5,7},{7,5},{8,10},{10,8},{9,1... | collective-permute-start | bytes 196616 | tf_op jit(solution)/shard_map/ppermute | solution.py:73
  96.3 10.7 %all-to-all-start.2 = ((bf16[16,48,128]{2,1,0:T(8,128)(2,1)}), bf16[16,48,128]{2,1,0:T(8,128)(2,1)S(1)}, u32[]{:S(2)}, u32[]{:S(2)}) async-start(bf16[16,48,128]{2,1,0:T(8,128)(2,1)} %bitcast.8), calls=%async_computation.2 | async-start | bytes 393216 | tf_op jit(solution)/shard_map/all_to_all | solution.py:85
  99.8 85.9 %all-gather.6.cloned.1.call-start = ((), (), s32[]{:S(2)}) async-start(), calls=%async_computation.5 | async-start | bytes 4456448 | tf_op jit(solution)/shard_map/all_gather | solution.py:100
  132.8 125.6 %all-gather.4.cloned.1.call-start = ((), (), s32[]{:S(2)}) async-start(), calls=%async_computation.4 | async-start | bytes 8912896 | tf_op jit(solution)/shard_map/all_gather | solution.py:32
  133.6 197.6 %all-gather.8.cloned.1.call-start = ((), (), s32[]{:S(2)}) async-start(), calls=%async_computation.6 | async-start | bytes 8912896 | tf_op jit(solution)/shard_map/all_gather | solution.py:33
  185.8 145.4 %collective-permute-start.4 = (bf16[2048,1024]{1,0:T(8,128)(2,1)}, bf16[2048,1024]{1,0:T(8,128)(2,1)}, u32[]{:S(2)}, u32[]{:S(2)}) collective-permute-start(bf16[2048,1024]{1,0:T(8,128)(2,1)} %all-gather.6.cloned.1.call-done), channel_id=1, source_target_pairs={{0,4},{4,0},{1,5},{5,1},{2,6},{6,2},{3,7},{7,3},{8,12},{12,8},{9,1... | collective-permute-start | bytes 12582920 | tf_op jit(solution)/shard_map/ppermute | solution.py:101
  331.2 16.0 %copy-start.1 = (bf16[1024,1024]{1,0:T(8,128)(2,1)S(1)}, bf16[1024,1024]{1,0:T(8,128)(2,1)}, u32[]{:S(2)}) copy-start(bf16[1024,1024]{1,0:T(8,128)(2,1)} %param.9) | copy-start | bytes 6291460
Sparse Core Ops, SparseCore 0:
  132.9 52.7 all-gather.5
  187.9 70.5 all-gather.3
  260.6 70.5 all-gather.7
where the time goes:
time: 354 us
  waiting for transfers between devices  229 us (65%)
  matrix products  46.7 us (13%)
  starting transfers between devices  22.4 us (6%)
  blocking collectives  21.1 us (6%)
  other arithmetic  17.3 us (5%)
  between operations  14 us (4%)
    all_gather x1, waiting for transfers between devices, on_device(): all_mine = lax.all_gather(mine, 'corpus', axis=0, tiled=True)  71.8 us
    all_gather x1, waiting for transfers between devices, on_device(): all_theirs = lax.all_gather(theirs, 'corpus', axis=0, tiled=True)  58.1 us
    all_gather x1, waiting for transfers between devices, on_device(): grad_mine = lax.all_gather(query_grad, 'corpus', axis=0, tiled=True)  51.5 us
    all_to_all x1, waiting for transfers between devices, on_device(): lax.all_to_all(send_queries.reshape(n_corpus, slots_each, cols), 'corpus'...  23.9 us
    all_to_all x1, blocking collectives, on_device(): lax.all_to_all(block_part.reshape(n_corpus, slots_each, cols), 'corpus',...  21.1 us
    dot_general x1, matrix products, on_device(): lax.dot_general(all_theirs, grad_theirs, across, preferred_element_type=j...  16 us
    dot_general x1, matrix products, on_device(): lax.dot_general(all_mine, grad_mine, across, preferred_element_type=jnp.f...  14.6 us
    all_to_all x1, waiting for transfers between devices, on_device(): lax.all_to_all(scores.reshape(n_corpus, slots_each, ROWS), 'corpus', 0, 0...  8.74 us
  transfers between devices with their start and end apart: 11, of which 10 were waited for; matrix products, arithmetic and copies ran while one was open for 5% of the time, Pallas kernels for 0%

commit v1 on v0

--- a/solution.py
+++ b/solution.py
@@ -97,7 +97,9 @@
     query_grad = lax.dot_general(
         owner, arrived, (((0,), (0,)), ((), ())), preferred_element_type=jnp.float32
     ).astype(jnp.bfloat16)
-    grad_mine = lax.all_gather(query_grad, "corpus", axis=0, tiled=True)
+    grad_mine = jnp.concatenate(
+        lax.all_to_all(jnp.stack([query_grad] * lax.axis_size("corpus")), "corpus", 0, 0), axis=0
+    )
     grad_theirs = lax.ppermute(grad_mine, "fsdp", SWAP)
     across = (((0,), (0,)), ((), ()))
     head_grad = lax.dot_general(

time: 354 us -> 273 us (0.77)
  waiting for transfers between devices: 229 us -> 53.8 us
  blocking collectives: 21.1 us -> 110 us
  starting transfers between devices: 22.4 us -> 27.2 us
    all_to_all x0 -> x1, blocking collectives: none -> 86.8 us  [on_device(): lax.all_to_all(jnp.stack([query_grad] * lax.axis_size('corpus')), 'corpus...]
    all_gather x1, waiting for transfers between devices: 71.8 us -> 0.01 us  [on_device(): all_mine = lax.all_gather(mine, 'corpus', axis=0, tiled=True)]
    all_gather x1, waiting for transfers between devices: 58.1 us -> 0.01 us  [on_device(): all_theirs = lax.all_gather(theirs, 'corpus', axis=0, tiled=True)]
    all_gather x1 -> x0, waiting for transfers between devices: 51.5 us -> none  [on_device(): grad_mine = lax.all_gather(query_grad, 'corpus', axis=0, tiled=True)]
    all_to_all x1, waiting for transfers between devices: 8.74 us -> 13.9 us  [on_device(): lax.all_to_all(scores.reshape(n_corpus, slots_each, ROWS), 'corpus', 0, 0...]
  transfers between devices with their start and end apart: 11 -> 10, of which waited for: 10 -> 7; matrix products, arithmetic and copies ran while one was open for 5% -> 18% of each run, Pallas kernels for 0% -> 0%
where the time goes in v1:
time: 273 us; the launch traced here: 272 us
  blocking collectives  110 us (40%)
  waiting for transfers between devices  53.8 us (20%)
  matrix products  46 us (17%)
  starting transfers between devices  27.2 us (10%)
  other arithmetic  17.4 us (6%)
  between operations  14.3 us (5%)
  local copies, waits for them, and re-layouts  3.19 us (1%)
    all_to_all x1, blocking collectives, on_device(): lax.all_to_all(jnp.stack([query_grad] * lax.axis_size('corpus')), 'corpus...  86.8 us
    all_to_all x1, waiting for transfers between devices, on_device(): lax.all_to_all(send_queries.reshape(n_corpus, slots_each, cols), 'corpus'...  24.9 us
    all_to_all x1, blocking collectives, on_device(): lax.all_to_all(block_part.reshape(n_corpus, slots_each, cols), 'corpus',...  23.6 us
    dot_general x1, matrix products, on_device(): lax.dot_general(all_theirs, grad_theirs, across, preferred_element_type=j...  16 us
    dot_general x1, matrix products, on_device(): lax.dot_general(all_mine, grad_mine, across, preferred_element_type=jnp.f...  14.6 us
    all_to_all x1, waiting for transfers between devices, on_device(): lax.all_to_all(scores.reshape(n_corpus, slots_each, ROWS), 'corpus', 0, 0...  13.9 us
    all_to_all x1, starting transfers between devices, on_device(): lax.all_to_all(send_queries.reshape(n_corpus, slots_each, cols), 'corpus'...  7.92 us
    all_to_all x1, waiting for transfers between devices, on_device(): lax.all_to_all(dense.reshape(n_corpus, slots_each, ROWS), 'corpus', 0, 0,...  7.13 us
  transfers between devices with their start and end apart: 10, of which 7 were waited for; matrix products, arithmetic and copies ran while one was open for 18% of the time, Pallas kernels for 0%

profile of v1, /device:TPU:1, one launch (start us, length us, event | category | flops | bytes accessed | tf_op | source)
XLA Modules:
  0.0 272.2 jit_solution(5163541715565156069)
XLA Ops:
  7.2 0.0 copy-start
  7.2 0.0 copy-start.6
  7.2 0.0 all-gather.3.cloned.1.call-start
  7.2 2.3 broadcast_select_fusion
  9.5 0.0 all-gather.3.cloned.1.call-update
  9.5 1.5 collective-permute-start
  11.0 0.1 copy.18
  11.1 0.1 eq.213
  11.2 1.3 collective-permute-done
  12.5 3.9 %fusion.26 = f32[128,1024]{1,0:T(8,128)} fusion(bf16[128,2048]{1,0:T(8,128)(2,1)S(1)} %collective-permute-done, bf16[2048,1024]{1,0:T(8,128)(2,1)} %param.8), kind=kOutput, calls=%fused_computation.91 | convolution fusion | flops 536870912 | bytes 5242880 | tf_op jit(solution)/shard_map/dot_general | solution.py:28
  16.5 0.4 collective-permute-start.1
  16.9 0.0 copy-done.7
  16.9 0.2 select_reduce_fusion.2
  17.1 0.3 fusion.2
  17.4 0.1 add.152
  17.5 0.2 slice_reduce_fusion.3
  17.8 1.0 collective-permute-done.1
  18.7 4.6 %convolution_convert_fusion = bf16[768,1024]{1,0:T(8,128)(2,1)} fusion(f32[128,1024]{1,0:T(8,128)} %collective-permute-done.1, s32[128]{0:T(128)S(1)} %get-tuple-element.3, s32[128]{0:T(128)S(1)} %get-tuple-element.4, s32[128]{0:T(128)S(1)} %get-tuple-element.5, s32[128]{0:T(128)S(1)} %get-tuple-element.2, bf16[128,2048]{1,0:T(8,128)(2,1)S(1)} %copy-done.2, ...), kind=kOutput, calls=%fused_computation.5 | convolution fusion | flops 739934208 | bytes 6817792 | tf_op jit(solution)/shard_map/dot_general | solution.py:53
  23.3 7.9 %all-to-all-start = ((bf16[16,48,1024]{2,1,0:T(8,128)(2,1)}), bf16[16,48,1024]{2,1,0:T(8,128)(2,1)}, u32[]{:S(2)}, u32[]{:S(2)}) async-start(bf16[16,48,1024]{2,1,0:T(8,128)(2,1)} %bitcast.47), calls=%async_computation | async-start | bytes 3145728 | tf_op jit(solution)/shard_map/all_to_all | solution.py:54
  31.3 0.0 all-gather.5.cloned.1.call-start
  31.3 0.7 all-gather.5.cloned.1.call-update
  32.1 24.9 %all-to-all-done = bf16[16,48,1024]{2,1,0:T(8,128)(2,1)} async-done(((bf16[16,48,1024]{2,1,0:T(8,128)(2,1)}), bf16[16,48,1024]{2,1,0:T(8,128)(2,1)}, u32[]{:S(2)}, u32[]{:S(2)}) %all-to-all-start) | async-done | bytes 1572896 | tf_op jit(solution)/shard_map/all_to_all | solution.py:54
  57.0 0.0 copy-done
  57.0 3.2 %fusion.27 = f32[768,1024]{1,0:T(8,128)S(1)} fusion(bf16[768,1024]{1,0:T(8,128)(2,1)} %bitcast.3, bf16[1024,1024]{1,0:T(8,128)(2,1)S(1)} %copy-done), kind=kOutput, calls=%fused_computation.92 | convolution fusion | flops 1610612736 | bytes 6815744 | tf_op jit(solution)/shard_map/dot_general | solution.py:57
  60.2 0.0 copy-start.5
  60.2 0.0 copy-start.4
  60.3 2.1 fusion.9
  62.4 5.7 %all-to-all-start.1 = ((f32[16,48,128]{2,1,0:T(8,128)}), f32[16,48,128]{2,1,0:T(8,128)S(1)}, u32[]{:S(2)}, u32[]{:S(2)}) async-start(f32[16,48,128]{2,1,0:T(8,128)} %bitcast.4), calls=%async_computation.1 | async-start | bytes 786432 | tf_op jit(solution)/shard_map/all_to_all | solution.py:63
  68.1 0.0 copy-done.5
  68.1 0.1 copy.17
  68.2 0.0 copy-done.4
  68.3 13.9 %all-to-all-done.1 = f32[16,48,128]{2,1,0:T(8,128)S(1)} async-done(((f32[16,48,128]{2,1,0:T(8,128)}), f32[16,48,128]{2,1,0:T(8,128)S(1)}, u32[]{:S(2)}, u32[]{:S(2)}) %all-to-all-start.1) | async-done | bytes 393248 | tf_op jit(solution)/shard_map/all_to_all | solution.py:63
  82.2 1.0 gather_fusion
  83.2 5.1 %select_reduce_fusion.1 = f32[512,32]{1,0:T(8,128)S(1)} fusion(f32[512,128]{1,0:T(8,128)S(1)} %gather_fusion, s32[512,32]{1,0:T(8,128)S(1)} %bitcast.48), kind=kLoop, calls=%fused_computation.2 | loop fusion | flops 6275072 | bytes 393216 | tf_op jit(solution)/shard_map/reduce_sum | solution.py:70
  88.3 0.1 reshape.201
  88.4 0.1 copy.20
  88.5 1.2 collective-permute-start.2
  89.8 2.3 collective-permute-done.2
  92.2 2.6 collective-permute-start.3
  94.8 2.6 collective-permute-done.3
  97.5 0.6 fusion.18
  98.0 0.1 copy.21
  98.1 0.1 reshape.207
  98.3 5.6 %select_reduce_fusion = bf16[512,128]{1,0:T(8,128)(2,1)S(1)} fusion(f32[512,32]{1,0:T(8,128)S(1)} %reshape.207, s32[512,32]{1,0:T(8,128)S(1)} %bitcast.49), kind=kLoop, calls=%fused_computation.1 | loop fusion | flops 6225920 | bytes 262144 | tf_op jit(solution)/shard_map/reduce_sum | solution.py:81
  103.9 1.1 fusion.1
  105.0 3.5 %all-to-all-start.2 = ((bf16[16,48,128]{2,1,0:T(8,128)(2,1)}), bf16[16,48,128]{2,1,0:T(8,128)(2,1)S(1)}, u32[]{:S(2)}, u32[]{:S(2)}) async-start(bf16[16,48,128]{2,1,0:T(8,128)(2,1)} %bitcast.8), calls=%async_computation.2 | async-start | bytes 393216 | tf_op jit(solution)/shard_map/all_to_all | solution.py:85
  108.5 7.1 %all-to-all-done.2 = bf16[16,48,128]{2,1,0:T(8,128)(2,1)S(1)} async-done(((bf16[16,48,128]{2,1,0:T(8,128)(2,1)}), bf16[16,48,128]{2,1,0:T(8,128)(2,1)S(1)}, u32[]{:S(2)}, u32[]{:S(2)}) %all-to-all-start.2) | async-done | bytes 196640 | tf_op jit(solution)/shard_map/all_to_all | solution.py:85
  115.6 1.2 bitcast_select_fusion
  116.9 0.1 constant_dynamic-update-slice_fusion.6
  116.9 0.1 constant_dynamic-update-slice_fusion.5
  117.0 0.1 constant_dynamic-update-slice_fusion.4
  117.1 0.1 constant_dynamic-update-slice_fusion.3
  117.1 0.1 constant_dynamic-update-slice_fusion.2
  117.2 0.1 constant_dynamic-update-slice_fusion.1
  117.3 0.1 constant_dynamic-update-slice_fusion
  117.4 1.8 convolution_convert_fusion.1
  119.2 23.6 %all_to_all.25 = bf16[16,48,1024]{2,1,0:T(8,128)(2,1)S(1)} all-to-all(bf16[16,48,1024]{2,1,0:T(8,128)(2,1)S(1)} %bitcast.51), channel_id=1, replica_groups=mesh['corpus'=16,'fsdp'=2,'tensor'=4] {'corpus'}, dimensions={0} | all-to-all | bytes 3145728 | tf_op jit(solution)/shard_map/all_to_all | solution.py:94
  142.7 0.4 convolution_convert_fusion.2
  143.2 0.5 stack.2
  143.7 86.8 %all_to_all.26 = bf16[16,128,1024]{2,1,0:T(8,128)(2,1)} all-to-all(bf16[16,128,1024]{2,1,0:T(8,128)(2,1)S(1)} %stack.2), channel_id=1, replica_groups=mesh['corpus'=16,'fsdp'=2,'tensor'=4] {'corpus'}, dimensions={0} | all-to-all | bytes 8388608 | tf_op jit(solution)/shard_map/all_to_all | solution.py:101
  230.5 4.3 %collective-permute-start.4 = (bf16[2048,1024]{1,0:T(8,128)(2,1)}, bf16[2048,1024]{1,0:T(8,128)(2,1)}, u32[]{:S(2)}, u32[]{:S(2)}) collective-permute-start(bf16[2048,1024]{1,0:T(8,128)(2,1)} %bitcast.12), channel_id=1, source_target_pairs={{0,4},{4,0},{1,5},{5,1},{2,6},{6,2},{3,7},{7,3},{8,12},{12,8},{9,1... | collective-permute-start | bytes 12582920 | tf_op jit(solution)/shard_map/ppermute | solution.py:103
  234.8 14.6 %fusion.28 = f32[2048,1024]{1,0:T(8,128)} fusion(bf16[2048,2048]{1,0:T(8,128)(2,1)} %all-gather.3.cloned.1.call-done, bf16[2048,1024]{1,0:T(8,128)(2,1)} %bitcast.12), kind=kOutput, calls=%fused_computation.93 | convolution fusion | flops 8589934592 | bytes 20971520 | tf_op jit(solution)/shard_map/dot_general | solution.py:105
  249.4 0.0 collective-permute-done.4
  249.4 16.0 %convolution_add_fusion = f32[2048,1024]{1,0:T(8,128)} fusion(f32[2048,1024]{1,0:T(8,128)} %fusion.28, bf16[2048,2048]{1,0:T(8,128)(2,1)} %all-gather.5.cloned.1.call-done, bf16[2048,1024]{1,0:T(8,128)(2,1)} %collective-permute-done.4), kind=kOutput, calls=%fused_computation.4 | convolution fusion | flops 8592031744 | bytes 29360128 | tf_op jit(solution)/shard_map/dot_general | solution.py:107
  (28 shorter events, 0.4 us)
Async XLA Ops:
  7.2 49.8 %copy-start = (bf16[1024,1024]{1,0:T(8,128)(2,1)S(1)}, bf16[1024,1024]{1,0:T(8,128)(2,1)}, u32[]{:S(2)}) copy-start(bf16[1024,1024]{1,0:T(8,128)(2,1)} %param.9) | copy-start | bytes 6291460
  7.2 3.8 %copy-start.6 = (s32[128,4]{0,1:T(4,128)S(1)}, s32[128,4]{0,1:T(4,128)}, u32[]{:S(2)}) copy-start(s32[128,4]{0,1:T(4,128)} %param.11) | copy-start | bytes 6148
  7.2 227.6 %all-gather.3.cloned.1.call-start = ((), (), s32[]{:S(2)}) async-start(), calls=%async_computation.5 | async-start | bytes 8912896 | tf_op jit(solution)/shard_map/all_gather | solution.py:32
  9.5 3.0 %collective-permute-start = (bf16[128,2048]{1,0:T(8,128)(2,1)S(1)}, bf16[128,2048]{1,0:T(8,128)(2,1)S(1)}, u32[]{:S(2)}, u32[]{:S(2)}) collective-permute-start(bf16[128,2048]{1,0:T(8,128)(2,1)S(1)} %get-tuple-element.8), channel_id=1, source_target_pairs={{0,4},{4,0},{1,5},{5,1},{2,6},{6,2},{3,7},{7,3},{8,12},{12,8},{9,1... | collective-permute-start | bytes 1572872 | tf_op jit(solution)/shard_map/ppermute | solution.py:27
  12.5 3.9 %copy-start.3 = (bf16[128,2048]{1,0:T(8,128)(2,1)}, bf16[128,2048]{1,0:T(8,128)(2,1)S(1)}, u32[]{:S(2)}) copy-start(bf16[128,2048]{1,0:T(8,128)(2,1)S(1)} %collective-permute-done) | copy-start | bytes 1572868
  12.5 4.3 %copy-start.7 = (s32[128]{0:T(128)S(1)}, s32[128]{0:T(128)}, u32[]{:S(2)}) copy-start(s32[128]{0:T(128)} %param.13) | copy-start | bytes 1540
  12.5 6.2 %copy-start.2 = (bf16[128,2048]{1,0:T(8,128)(2,1)S(1)}, bf16[128,2048]{1,0:T(8,128)(2,1)}, u32[]{:S(2)}) copy-start(bf16[128,2048]{1,0:T(8,128)(2,1)} %get-tuple-element.9) | copy-start | bytes 1572868
  16.5 2.3 collective-permute-start.1
  23.3 33.6 %all-to-all-start = ((bf16[16,48,1024]{2,1,0:T(8,128)(2,1)}), bf16[16,48,1024]{2,1,0:T(8,128)(2,1)}, u32[]{:S(2)}, u32[]{:S(2)}) async-start(bf16[16,48,1024]{2,1,0:T(8,128)(2,1)} %bitcast.47), calls=%async_computation | async-start | bytes 3145728 | tf_op jit(solution)/shard_map/all_to_all | solution.py:54
  31.3 218.1 %all-gather.5.cloned.1.call-start = ((), (), s32[]{:S(2)}) async-start(), calls=%async_computation.6 | async-start | bytes 8912896 | tf_op jit(solution)/shard_map/all_gather | solution.py:33
  60.2 7.8 %copy-start.5 = (s32[128,4,32]{0,2,1:T(8,128)S(1)}, s32[128,4,32]{0,2,1:T(8,128)}, u32[]{:S(2)}) copy-start(s32[128,4,32]{0,2,1:T(8,128)} %param.12) | copy-start | bytes 196612
  60.2 8.0 %copy-start.4 = (f32[128,4,32]{0,2,1:T(8,128)S(1)}, f32[128,4,32]{0,2,1:T(8,128)}, u32[]{:S(2)}) copy-start(f32[128,4,32]{0,2,1:T(8,128)} %param.10) | copy-start | bytes 196612
  62.4 19.8 %all-to-all-start.1 = ((f32[16,48,128]{2,1,0:T(8,128)}), f32[16,48,128]{2,1,0:T(8,128)S(1)}, u32[]{:S(2)}, u32[]{:S(2)}) async-start(f32[16,48,128]{2,1,0:T(8,128)} %bitcast.4), calls=%async_computation.1 | async-start | bytes 786432 | tf_op jit(solution)/shard_map/all_to_all | solution.py:63
  88.5 3.6 %collective-permute-start.2 = (f32[128,128]{0,1:T(8,128)S(1)}, f32[128,128]{0,1:T(8,128)S(1)}, u32[]{:S(2)}, u32[]{:S(2)}) collective-permute-start(f32[128,128]{0,1:T(8,128)S(1)} %copy.20), channel_id=1, source_target_pairs={{0,1},{1,0},{2,3},{3,2},{4,5},{5,4},{6,7},{7,6},{8,9},{9,8},{10,11... | collective-permute-start | bytes 196616 | tf_op jit(solution)/shard_map/ppermute | solution.py:72
  92.2 5.2 %collective-permute-start.3 = (f32[128,128]{0,1:T(8,128)S(1)}, f32[128,128]{0,1:T(8,128)S(1)}, u32[]{:S(2)}, u32[]{:S(2)}) collective-permute-start(f32[128,128]{0,1:T(8,128)S(1)} %add.157), channel_id=1, source_target_pairs={{0,2},{2,0},{1,3},{3,1},{4,6},{6,4},{5,7},{7,5},{8,10},{10,8},{9,1... | collective-permute-start | bytes 196616 | tf_op jit(solution)/shard_map/ppermute | solution.py:73
  105.0 10.7 %all-to-all-start.2 = ((bf16[16,48,128]{2,1,0:T(8,128)(2,1)}), bf16[16,48,128]{2,1,0:T(8,128)(2,1)S(1)}, u32[]{:S(2)}, u32[]{:S(2)}) async-start(bf16[16,48,128]{2,1,0:T(8,128)(2,1)} %bitcast.8), calls=%async_computation.2 | async-start | bytes 393216 | tf_op jit(solution)/shard_map/all_to_all | solution.py:85
  230.5 18.9 %collective-permute-start.4 = (bf16[2048,1024]{1,0:T(8,128)(2,1)}, bf16[2048,1024]{1,0:T(8,128)(2,1)}, u32[]{:S(2)}, u32[]{:S(2)}) collective-permute-start(bf16[2048,1024]{1,0:T(8,128)(2,1)} %bitcast.12), channel_id=1, source_target_pairs={{0,4},{4,0},{1,5},{5,1},{2,6},{6,2},{3,7},{7,3},{8,12},{12,8},{9,1... | collective-permute-start | bytes 12582920 | tf_op jit(solution)/shard_map/ppermute | solution.py:103
  249.4 16.0 %copy-start.1 = (bf16[1024,1024]{1,0:T(8,128)(2,1)S(1)}, bf16[1024,1024]{1,0:T(8,128)(2,1)}, u32[]{:S(2)}) copy-start(bf16[1024,1024]{1,0:T(8,128)(2,1)} %param.9) | copy-start | bytes 6291460
Sparse Core Ops, SparseCore 0:
  10.1 92.1 all-gather.2
  104.5 127.2 all-gather.4
